TPU v7x, 32 devices: a whole 2x2x4 slice. The times are simulated.
32 devices in a mesh: member: 2 (over y), wave: 4 (over z), level: 2 (over x), fld: 2 (over core).
Axes of the slice: x: 2, y: 2, z: 4, core: 2. Of those that a mesh axis runs over, the one named last changes fastest.
Arguments:
- grid_state: bfloat16 [256, 2, 256, 1536], P(('member', 'level'), 'fld', 'wave'), parts along dimension 0, may hold values from -6 to 6
- legendre: bfloat16 [512, 2, 256, 256], P(('wave', 'level'), 'fld'), may hold values from -0.375 to 0.375
- wave_order: int32 [512], replicated, may hold values from 0 to 511, each once
- lat_order: int32 [256], replicated, may hold values from 0 to 255, each once
- eig_rates: float32 [128], replicated, may hold values from 0.1 to 4
- modes_in: bfloat16 [128, 128], replicated, may hold values from -0.5 to 0.5
- modes_out: bfloat16 [128, 128], replicated, may hold values from -0.5 to 0.5
Outputs:
- new_state: bfloat16 [256, 2, 256, 1536], P(('member', 'level'), 'fld', 'wave'), parts along dimension 0
There are 2 independent parts, one for each index of `member`. A program takes and returns all parts, laid end to end along the dimension named above; an argument that names none is the same for every part. Nothing has to cross between parts.
Inputs may be any that keep to these rules, and one draw needn't show every extreme that they name: Slot s holds zonal wavenumber wave_order[s]; every wavenumber 0 to 511 is held by exactly one slot. Latitude row r lies at Gaussian latitude index lat_order[r] counted from the equator, the same in both hemispheres; every index appears once.
All inputs are finite; a program needn't handle non-finite values.
Results may differ from a plain program's by a relative error of at most 0.0098.
Values may be sent and summed in bfloat16 or wider, within the bound.
No kernel may reach another device: no remote copies, remote signals or barrier semaphores. Data moves between devices by JAX's collectives and lax.ppermute only.
A program may use at most 128 MiB of HBM per device.

v0:
```python
import math
import jax
import jax.numpy as jnp
from jax import lax
from jax.sharding import PartitionSpec as P

tau_scale = 2.0


def partner(value, axis, stride):
    mask = 2**stride
    pairs = [(source, source ^ mask) for source in range(lax.axis_size(axis))]
    return lax.ppermute(value, axis, pairs)


def fourier_table(wave_order, lon_count):
    longitude = jnp.arange(lon_count, dtype=jnp.int32)
    phase_index = longitude[:, None] * wave_order[None, :] % lon_count
    angles = phase_index.astype(jnp.float32) * (2.0 * math.pi / lon_count)
    weight_scale = math.sqrt(2.0 / lon_count)
    return jnp.concatenate(
        [jnp.cos(angles) * weight_scale, -jnp.sin(angles) * weight_scale], axis=1
    ).astype(jnp.bfloat16)


def degrees(wave_ids, parity, half_count):
    return wave_ids[:, None] + 2 * jnp.arange(half_count, dtype=jnp.int32)[None, :] + parity


def triangle_mask(wave_ids, parity, half_count, wave_count):
    return (degrees(wave_ids, parity, half_count) <= wave_count - 1).astype(jnp.float32)


def damping(wave_ids, parity, half_count, wave_count, eig_rates):
    degree_f = degrees(wave_ids, parity, half_count).astype(jnp.float32)
    damp_ratio = tau_scale * degree_f * (degree_f + 1.0) / float(wave_count * (wave_count - 1))
    return 1.0 / (1.0 + damp_ratio[:, :, None] * eig_rates[None, None, :])


def forward_legendre(mirrored, table_part, in_triangle):
    spectral = jnp.einsum(
        "lhrcs,shrj->sjcl", mirrored, table_part, preferred_element_type=jnp.float32
    )
    return (spectral * in_triangle[:, :, None, None]).astype(jnp.bfloat16)


def inverse_legendre(solved, table_part):
    return jnp.einsum(
        "sjcl,shrj->lhrcs", solved, table_part, preferred_element_type=jnp.float32
    ).astype(jnp.bfloat16)


def implicit_solve(columns, factor, modes_in, modes_out):
    modal = jnp.einsum("sjcl,kl->sjck", columns, modes_in, preferred_element_type=jnp.float32)
    modal = (modal * factor[:, :, None, :]).astype(jnp.bfloat16)
    return jnp.einsum("sjck,lk->sjcl", modal, modes_out, preferred_element_type=jnp.float32).astype(
        jnp.bfloat16
    )


def shards(grid_state, legendre, wave_order, lat_order, eig_rates, modes_in, modes_out):
    lon_count = grid_state.shape[3]
    rows_here = grid_state.shape[2]
    wave_count = wave_order.shape[0]
    half_rows = lat_order.shape[0]
    half_count = legendre.shape[3]
    wave_size = lax.axis_size("wave")
    level_size = lax.axis_size("level")
    parity = lax.axis_index("fld")
    wave_place = lax.axis_index("wave")
    level_place = lax.axis_index("level")
    wave_table = fourier_table(wave_order, lon_count)
    lat_rows = lax.dynamic_slice_in_dim(lat_order, wave_place * rows_here, rows_here)
    sine = jnp.sin((lat_rows.astype(jnp.float32) + 0.5) * (math.pi / (2.0 * half_rows)))
    hemi_sign = 1.0 - 2.0 * parity.astype(jnp.float32)
    coupling = (0.5 * hemi_sign * sine)[None, None, :, None]
    wide_count = wave_count // wave_size
    narrow_count = wide_count // level_size
    wide_start = wave_place * wide_count
    narrow_start = wide_start + level_place * narrow_count
    wide_waves = lax.dynamic_slice_in_dim(wave_order, wide_start, wide_count)
    narrow_waves = lax.dynamic_slice_in_dim(wave_order, narrow_start, narrow_count)
    factor = damping(narrow_waves, parity, half_count, wave_count, eig_rates)
    wide_table = lax.all_gather(legendre, "level", axis=0, tiled=True)
    wide_mask = triangle_mask(wide_waves, parity, half_count, wave_count)
    initial = grid_state.astype(jnp.float32)
    current = grid_state
    forcing = (initial + coupling * jnp.tanh(current.astype(jnp.float32))).astype(jnp.bfloat16)
    fourier_rows = jnp.einsum(
        "lhrg,gk->lhrk", forcing, wave_table, preferred_element_type=jnp.float32
    )
    fourier_rows = fourier_rows.astype(jnp.bfloat16).reshape(
        fourier_rows.shape[:3] + (2, wave_count)
    )
    mirror_part = partner(fourier_rows, "fld", 0)
    mirrored = (
        mirror_part.astype(jnp.float32) + hemi_sign * fourier_rows.astype(jnp.float32)
    ).astype(jnp.bfloat16)
    gathered = lax.all_to_all(mirrored, "wave", split_axis=4, concat_axis=2, tiled=True)
    spectral = forward_legendre(gathered, wide_table, wide_mask)
    columns = lax.all_to_all(spectral, "level", split_axis=0, concat_axis=3, tiled=True)
    solved = implicit_solve(columns, factor, modes_in, modes_out)
    level_rows = lax.all_to_all(solved, "level", split_axis=3, concat_axis=0, tiled=True)
    grid_coeffs = inverse_legendre(level_rows, wide_table)
    grid_coeffs = lax.all_to_all(grid_coeffs, "wave", split_axis=2, concat_axis=4, tiled=True)
    mirror_back = partner(grid_coeffs, "fld", 0)
    hemi_grid = (
        0.5 * (mirror_back.astype(jnp.float32) + hemi_sign * grid_coeffs.astype(jnp.float32))
    ).astype(jnp.bfloat16)
    flat_coeffs = hemi_grid.reshape(hemi_grid.shape[:3] + (2 * wave_count,))
    current = jnp.einsum(
        "lhrk,gk->lhrg", flat_coeffs, wave_table, preferred_element_type=jnp.float32
    ).astype(jnp.bfloat16)
    return current


def solution(mesh):
    placed = (
        P(("member", "level"), "fld", "wave", None),
        P(("wave", "level"), "fld", None, None),
        P(),
        P(),
        P(),
        P(),
        P(),
    )
    return jax.shard_map(
        shards,
        mesh=mesh,
        in_specs=placed,
        out_specs=P(("member", "level"), "fld", "wave", None),
        check_vma=False,
    )
```

profile of v0, /device:TPU:0, one launch (start us, length us, event | category | flops | bytes accessed | tf_op | source)
XLA Modules:
  0.0 995.7 jit_solution(6568454296517900749)
XLA Ops:
  6.5 0.0 copy-start
  6.5 0.0 all-gather.2.cloned.1.call-start
  6.5 14.1 %multiply_convert_fusion.4 = (bf16[1536,512]{1,0:T(8,128)(2,1)S(1)}, bf16[1536,512]{1,0:T(8,128)(2,1)S(1)}) fusion(s32[512]{0:T(512)} %param.9), kind=kLoop, calls=%fused_computation.28 | loop fusion | flops 11010048 | bytes 3147776 | tf_op jit(solution)/shard_map/convert
  20.6 0.0 copy-start.2
  20.7 0.8 sine_multiply_fusion
  21.5 18.9 %fusion.13 = bf16[64,64,1024]{2,1,0:T(8,128)(2,1)} fusion(bf16[64,1,64,1536]{3,2,1,0:T(8,128)(2,1)} %param.7, f32[64]{0:T(128)S(1)} %sine_multiply_fusion, bf16[1536,512]{1,0:T(8,128)(2,1)S(1)} %get-tuple-element.6, bf16[1536,512]{1,0:T(8,128)(2,1)S(1)} %get-tuple-element.5), kind=kOutput, calls=%fused_computation.21 | convolution fusion | flops 12920553472 | bytes 24117504 | tf_op jit(solution)/shard_map/lhrg,gk->lhrk/dot_general | solution.py:89
  40.4 14.5 %reshape.138 = bf16[64,1,64,2,512]{4,3,2,0,1:T(2,128)(2,1)} reshape(bf16[64,64,1024]{2,1,0:T(8,128)(2,1)} %fusion.13) | data formatting | bytes 16777216 | tf_op jit(solution)/shard_map/reshape | solution.py:92
  54.9 9.0 copy.61
  64.0 0.5 collective-permute-start
  64.5 0.0 all-gather.2.cloned.1.call-update
  64.5 13.1 %collective-permute-done = bf16[64,1,64,2,512]{4,2,3,0,1:T(8,128)(2,1)} collective-permute-done((bf16[64,1,64,2,512]{4,2,3,0,1:T(8,128)(2,1)}, bf16[64,1,64,2,512]{4,2,3,0,1:T(8,128)(2,1)}, u32[]{:S(2)}, u32[]{:S(2)}) %collective-permute-start) | collective-permute-done | bytes 8388640 | tf_op jit(solution)/shard_map/ppermute | solution.py:13
  77.6 12.1 %add_convert_fusion = bf16[64,1,64,2,512]{4,2,3,0,1:T(8,128)(2,1)} fusion(bf16[64,1,64,2,512]{4,2,3,0,1:T(8,128)(2,1)} %collective-permute-done, f32[]{:T(128)S(6)} %sub.3, bf16[64,1,64,2,512]{4,3,2,0,1:T(2,128)(2,1)} %reshape.138), kind=kLoop, calls=%fused_computation.11 | loop fusion | flops 20971520 | bytes 25165828 | tf_op jit(solution)/shard_map/convert_element_type | solution.py:98
  89.7 34.4 %copy.63 = bf16[64,1,64,2,512]{2,3,0,1,4:T(2,128)(2,1)} copy(bf16[64,1,64,2,512]{4,2,3,0,1:T(8,128)(2,1)} %add_convert_fusion) | data formatting | bytes 16777216 | tf_op jit(solution)/shard_map/convert_element_type | solution.py:98
  124.1 16.8 %reshape.146 = bf16[4,2,524288]{2,1,0:T(2,128)(2,1)} reshape(bf16[512,1,64,2,64]{4,3,2,1,0:T(2,128)(2,1)} %bitcast.76) | data formatting | bytes 16777216
  140.9 6.2 all-to-all-start
  147.2 0.1 dynamic_slice.10
  147.2 0.1 fusion.26
  147.3 184.2 %all-to-all-done = bf16[4,2,524288]{2,1,0:T(2,128)(2,1)} async-done(((bf16[4,2,524288]{2,1,0:T(2,128)(2,1)}), bf16[4,2,524288]{2,1,0:T(2,128)(2,1)}, u32[]{:S(2)}, u32[]{:S(2)}) %all-to-all-start) | async-done | bytes 8388640 | tf_op jit(solution)/shard_map/all_to_all | solution.py:99
  331.6 16.0 %reshape.147 = bf16[512,1,64,2,64]{4,3,2,1,0:T(2,128)(2,1)} reshape(bf16[4,2,524288]{2,1,0:T(2,128)(2,1)} %all-to-all-done) | data formatting | bytes 16777216
  347.5 41.2 %copy.81 = bf16[64,1,64,2,4,128]{5,4,2,3,0,1:T(4,128)(2,1)} copy(bf16[64,1,64,2,4,128]{2,3,0,5,4,1:T(2,128)(2,1)} %bitcast.77) | data formatting | bytes 16777216 | tf_op jit(solution)/shard_map/all_to_all | solution.py:99
  388.7 9.3 copy.65
  398.0 12.1 %copy.66 = bf16[64,256,2,128]{1,0,2,3:T(8,128)(2,1)} copy(bf16[64,256,2,128]{3,1,2,0:T(8,128)(2,1)} %bitcast.81) | data formatting | bytes 16777216 | tf_op jit(solution)/shard_map/reshape.6
  410.1 15.1 %fusion.18 = bf16[128,256,2,64]{1,3,2,0:T(8,128)(2,1)} fusion(f32[128,256]{1,0:T(8,128)S(1)} %fusion.26, bf16[64,256,2,128]{1,0,2,3:T(8,128)(2,1)} %copy.66, bf16[128,1,256,256]{3,2,1,0:T(8,128)(2,1)} %all-gather.2.cloned.1.call-done), kind=kOutput, calls=%fused_computation.22 | convolution fusion | flops 2155872256 | bytes 33685504 | tf_op jit(solution)/shard_map/lhrcs,shrj->sjcl/dot_general | solution.py:41
  425.2 7.1 all-to-all-start.1
  432.4 0.1 dynamic_slice.11
  432.4 0.1 multiply_multiply_fusion
  432.5 0.0 copy-done.8
  432.5 15.2 %add_divide_fusion = f32[64,256,128]{2,1,0:T(8,128)} fusion(f32[128]{0:T(128)S(1)} %copy-done.8, f32[64,256]{1,0:T(8,128)S(1)} %multiply_multiply_fusion), kind=kLoop, calls=%fused_computation.19 | loop fusion | flops 6291456 | bytes 8454656 | tf_op jit(solution)/shard_map/div | solution.py:37
  447.7 77.0 %all-to-all-done.1 = bf16[128,256,2,64]{1,3,2,0:T(8,128)(2,1)} async-done(((bf16[128,256,2,64]{1,3,2,0:T(8,128)(2,1)}), bf16[128,256,2,64]{1,3,2,0:T(8,128)(2,1)}, u32[]{:S(2)}, u32[]{:S(2)}) %all-to-all-start.1) | async-done | bytes 8388640 | tf_op jit(solution)/shard_map/all_to_all | solution.py:101
  524.7 8.4 copy.67
  533.1 0.0 copy-done
  533.1 10.6 %convolution_convert_fusion.1 = bf16[64,256,2,128]{3,1,2,0:T(8,128)(2,1)} fusion(bf16[64,256,2,128]{1,3,2,0:T(8,128)(2,1)} %bitcast.79, f32[64,256,128]{2,1,0:T(8,128)} %add_divide_fusion, bf16[128,128]{1,0:T(8,128)(2,1)S(1)} %copy-done, bf16[128,128]{1,0:T(8,128)(2,1)S(1)} %copy-done.6), kind=kOutput, calls=%fused_computation.20 | convolution fusion | flops 2160066560 | bytes 25231360 | tf_op jit(solution)/shard_map/sjck,lk->sjcl/dot_general | solution.py:56
  543.7 21.1 %copy.69 = bf16[64,256,2,128]{1,2,0,3:T(2,128)(2,1)} copy(bf16[64,256,2,128]{3,1,2,0:T(8,128)(2,1)} %convolution_convert_fusion.1) | data formatting | bytes 16777216 | tf_op jit(solution)/shard_map/convert_element_type | solution.py:56
  564.7 102.5 %all_to_all.69 = bf16[64,256,2,128]{1,2,0,3:T(2,128)(2,1)} all-to-all(bf16[64,256,2,128]{1,2,0,3:T(2,128)(2,1)} %copy.69), channel_id=1, replica_groups=mesh['member'=2,'wave'=4,'level'=2,'fld'=2] {'level'}, dimensions={3} | all-to-all | bytes 16777216 | tf_op jit(solution)/shard_map/all_to_all | solution.py:103
  667.2 15.9 %copy.70 = bf16[64,256,2,128]{1,3,2,0:T(8,128)(2,1)} copy(bf16[64,256,2,128]{1,2,0,3:T(2,128)(2,1)} %all_to_all.69) | data formatting | bytes 16777216 | tf_op jit(solution)/shard_map/all_to_all | solution.py:103
  683.2 8.3 copy.71
  691.5 13.3 %convert_bitcast_fusion = bf16[64,1,256,2,128]{2,0,3,4,1:T(8,128)(2,1)} fusion(bf16[128,256,2,64]{1,3,2,0:T(8,128)(2,1)} %bitcast.78, bf16[128,1,256,256]{3,2,1,0:T(8,128)(2,1)} %all-gather.2.cloned.1.call-done), kind=kOutput, calls=%fused_computation.18 | convolution fusion | flops 2151677952 | bytes 33554432 | tf_op jit(solution)/shard_map/sjcl,shrj->lhrcs/dot_general | solution.py:48
  704.7 13.5 %copy.72 = bf16[64,1,256,2,128]{4,0,3,1,2:T(8,128)(2,1)} copy(bf16[64,1,256,2,128]{2,0,3,4,1:T(8,128)(2,1)} %convert_bitcast_fusion) | data formatting | bytes 16777216 | tf_op jit(solution)/shard_map/convert_element_type | solution.py:50
  718.3 188.9 %all_to_all.70 = bf16[64,1,256,2,128]{4,0,3,1,2:T(8,128)(2,1)} all-to-all(bf16[64,1,256,2,128]{4,0,3,1,2:T(8,128)(2,1)} %copy.72), channel_id=1, replica_groups=mesh['member'=2,'wave'=4,'level'=2,'fld'=2] {'wave'}, dimensions={2} | all-to-all | bytes 16777216 | tf_op jit(solution)/shard_map/all_to_all | solution.py:105
  907.1 12.2 %copy.73 = bf16[64,1,256,2,128]{4,2,3,0,1:T(8,128)(2,1)} copy(bf16[64,1,256,2,128]{4,0,3,1,2:T(8,128)(2,1)} %all_to_all.70) | data formatting | bytes 16777216 | tf_op jit(solution)/shard_map/all_to_all | solution.py:105
  919.3 8.4 copy.87
  927.7 0.0 collective-permute-start.1
  927.7 13.4 %collective-permute-done.1 = bf16[64,1,64,2,512]{4,2,3,0,1:T(8,128)(2,1)S(1)} collective-permute-done((bf16[64,1,64,2,512]{4,2,3,0,1:T(8,128)(2,1)}, bf16[64,1,64,2,512]{4,2,3,0,1:T(8,128)(2,1)S(1)}, u32[]{:S(2)}, u32[]{:S(2)}) %collective-permute-start.1) | collective-permute-done | bytes 8388640 | tf_op jit(solution)/shard_map/ppermute | solution.py:13
  941.1 5.7 multiply_convert_fusion
  946.8 7.7 copy.75
  954.6 14.5 %reshape.141 = bf16[64,64,1024]{2,1,0:T(8,128)(2,1)} reshape(bf16[64,1,64,2,512]{4,3,2,0,1:T(2,128)(2,1)} %copy.75) | data formatting | bytes 16777216 | tf_op jit(solution)/shard_map/reshape.9
  969.1 0.0 copy-done.5
  969.1 19.4 %fusion.10 = bf16[64,1,64,1536]{3,2,1,0:T(8,128)(2,1)} fusion(bf16[64,64,1024]{2,1,0:T(8,128)(2,1)} %reshape.141, bf16[1536,512]{1,0:T(8,128)(2,1)S(1)} %copy-done.5, bf16[1536,512]{1,0:T(8,128)(2,1)S(1)} %copy-done.3), kind=kOutput, calls=%fused_computation.16 | convolution fusion | flops 12897484800 | bytes 24117248 | tf_op jit(solution)/shard_map/lhrk,gk->lhrg/dot_general | solution.py:111
  (15 shorter events, 0.0 us)
Async XLA Ops:
  6.5 526.6 %copy-start = (bf16[128,128]{1,0:T(8,128)(2,1)S(1)}, bf16[128,128]{1,0:T(8,128)(2,1)}, u32[]{:S(2)}) copy-start(bf16[128,128]{1,0:T(8,128)(2,1)} %param.13) | copy-start | bytes 98308
  6.5 403.6 %all-gather.2.cloned.1.call-start = ((), (), s32[]{:S(2)}) async-start(), calls=%async_computation.4 | async-start | bytes 25165824 | tf_op jit(solution)/shard_map/all_gather | solution.py:84
  20.6 19.8 %copy-start.2 = (bf16[1536,512]{1,0:T(8,128)(2,1)}, bf16[1536,512]{1,0:T(8,128)(2,1)S(1)}, u32[]{:S(2)}) copy-start(bf16[1536,512]{1,0:T(8,128)(2,1)S(1)} %get-tuple-element.5) | copy-start | bytes 4718596
  20.7 19.8 %copy-start.4 = (bf16[1536,512]{1,0:T(8,128)(2,1)}, bf16[1536,512]{1,0:T(8,128)(2,1)S(1)}, u32[]{:S(2)}) copy-start(bf16[1536,512]{1,0:T(8,128)(2,1)S(1)} %get-tuple-element.6) | copy-start | bytes 4718596
  64.0 13.6 %collective-permute-start = (bf16[64,1,64,2,512]{4,2,3,0,1:T(8,128)(2,1)}, bf16[64,1,64,2,512]{4,2,3,0,1:T(8,128)(2,1)}, u32[]{:S(2)}, u32[]{:S(2)}) collective-permute-start(bf16[64,1,64,2,512]{4,2,3,0,1:T(8,128)(2,1)} %copy.61), channel_id=1, source_target_pairs={{0,1},{1,0},{2,3},{3,2},{4,5},{5,4},{6,7},{7,6},{8,9},{9,8},{10,11... | collective-permute-start | bytes 25165832 | tf_op jit(solution)/shard_map/ppermute | solution.py:13
  140.9 6.2 copy-start.7
  140.9 190.6 %all-to-all-start = ((bf16[4,2,524288]{2,1,0:T(2,128)(2,1)}), bf16[4,2,524288]{2,1,0:T(2,128)(2,1)}, u32[]{:S(2)}, u32[]{:S(2)}) async-start(bf16[4,2,524288]{2,1,0:T(2,128)(2,1)} %reshape.146), calls=%async_computation | async-start | bytes 16777216 | tf_op jit(solution)/shard_map/all_to_all | solution.py:99
  425.2 7.3 copy-start.8
  425.2 99.4 %all-to-all-start.1 = ((bf16[128,256,2,64]{1,3,2,0:T(8,128)(2,1)}), bf16[128,256,2,64]{1,3,2,0:T(8,128)(2,1)}, u32[]{:S(2)}, u32[]{:S(2)}) async-start(bf16[128,256,2,64]{1,3,2,0:T(8,128)(2,1)} %fusion.18), calls=%async_computation.1 | async-start | bytes 16777216 | tf_op jit(solution)/shard_map/all_to_all | solution.py:101
  524.7 8.5 copy-start.6
  927.7 13.4 %collective-permute-start.1 = (bf16[64,1,64,2,512]{4,2,3,0,1:T(8,128)(2,1)}, bf16[64,1,64,2,512]{4,2,3,0,1:T(8,128)(2,1)S(1)}, u32[]{:S(2)}, u32[]{:S(2)}) collective-permute-start(bf16[64,1,64,2,512]{4,2,3,0,1:T(8,128)(2,1)} %bitcast.83), channel_id=1, source_target_pairs={{0,1},{1,0},{2,3},{3,2},{4,5},{5,4},{6,7},{7,6},{8,9},{9,8},{10,11... | collective-permute-start | bytes 25165832 | tf_op jit(solution)/shard_map/ppermute | solution.py:13
  954.6 14.5 %copy-start.3 = (bf16[1536,512]{1,0:T(8,128)(2,1)S(1)}, bf16[1536,512]{1,0:T(8,128)(2,1)}, u32[]{:S(2)}) copy-start(bf16[1536,512]{1,0:T(8,128)(2,1)} %copy-done.2) | copy-start | bytes 4718596
  954.6 14.5 %copy-start.5 = (bf16[1536,512]{1,0:T(8,128)(2,1)S(1)}, bf16[1536,512]{1,0:T(8,128)(2,1)}, u32[]{:S(2)}) copy-start(bf16[1536,512]{1,0:T(8,128)(2,1)} %copy-done.4) | copy-start | bytes 4718596
  969.1 19.4 %copy-start.1 = (bf16[128,128]{1,0:T(8,128)(2,1)S(1)}, bf16[128,128]{1,0:T(8,128)(2,1)}, u32[]{:S(2)}) copy-start(bf16[128,128]{1,0:T(8,128)(2,1)} %param.13) | copy-start | bytes 98308
Sparse Core Ops, SparseCore 0:
  64.6 201.2 all-gather.1
where the time goes:
time: 1010 us; the launch traced here: 996 us
  blocking collectives  291 us (29%)
  waiting for transfers between devices  288 us (29%)
  local copies, waits for them, and re-layouts  264 us (26%)
  matrix products  77.3 us (8%)
  other arithmetic  48.1 us (5%)
  between operations  13.9 us (1%)
  starting transfers between devices  13.8 us (1%)
    all_to_all x1, blocking collectives, shards(): lax.all_to_all(grid_coeffs, 'wave', split_axis=2, concat_axis=4, tiled=True)  189 us
    all_to_all x1, waiting for transfers between devices, shards(): lax.all_to_all(mirrored, 'wave', split_axis=4, concat_axis=2, tiled=True)  184 us
    all_to_all x1, blocking collectives, shards(): lax.all_to_all(solved, 'level', split_axis=3, concat_axis=0, tiled=True)  102 us
    all_to_all x1, waiting for transfers between devices, shards(): lax.all_to_all(spectral, 'level', split_axis=0, concat_axis=3, tiled=True)  77 us
    all_to_all x2, local copies, waits for them, and re-layouts, shards(): lax.all_to_all(mirrored, 'wave', split_axis=4, concat_axis=2, tiled=True)  50.5 us
    convert_element_type x1, local copies, waits for them, and re-layouts, shards(): mirrored = (mirror_part.astype(jnp.float32) + hemi_sign * fourier_rows.as...  34.4 us
    unnamed x20, local copies, waits for them, and re-layouts  32.8 us
    another operation x2, local copies, waits for them, and re-layouts  26.6 us
  transfers between devices with their start and end apart: 5, of which 4 were waited for; matrix products, arithmetic and copies ran while one was open for 16% of the time, Pallas kernels for 0%

commit v1 on v0

--- a/solution.py
+++ b/solution.py
@@ -5,6 +5,36 @@
 from jax.sharding import PartitionSpec as P
 
 tau_scale = 2.0
+
+
+def drive_terms(payload, dimension_no, packet):
+    y_new = payload.shape
+    arr_now = payload.reshape(
+        *y_new[:dimension_no], packet, y_new[dimension_no] // packet, *y_new[dimension_no + 1 :]
+    )
+    return jnp.moveaxis(arr_now, dimension_no, 0)
+
+
+def _wait_scenes(body, k_dim):
+    tall = list(body.shape[1:])
+    tall[k_dim] *= body.shape[0]
+    return jnp.moveaxis(body, 0, k_dim).reshape(tall)
+
+
+def try_all_the_tracks(a0, across, load, frame):
+    met_up = lax.axis_size(across)
+    t_next, r2 = (met_up, lax.axis_index(across))
+    left_arr = drive_terms(a0, load, t_next)
+    m = 1
+    queue = [left_arr[r2]]
+    while m < t_next:
+        v_next = left_arr[r2 ^ m]
+        piece_now = lax.ppermute(v_next, across, [(w, w ^ m) for w in range(t_next)])
+        queue.append(piece_now)
+        m = m + 1
+    vec_out = jnp.stack(queue, 0)
+    left_arr = vec_out[r2 ^ jnp.arange(t_next)]
+    return _wait_scenes(left_arr, frame)
 
 
 def partner(value, axis, stride):
@@ -96,7 +126,7 @@
     mirrored = (
         mirror_part.astype(jnp.float32) + hemi_sign * fourier_rows.astype(jnp.float32)
     ).astype(jnp.bfloat16)
-    gathered = lax.all_to_all(mirrored, "wave", split_axis=4, concat_axis=2, tiled=True)
+    gathered = try_all_the_tracks(mirrored, "wave", 4, 2)
     spectral = forward_legendre(gathered, wide_table, wide_mask)
     columns = lax.all_to_all(spectral, "level", split_axis=0, concat_axis=3, tiled=True)
     solved = implicit_solve(columns, factor, modes_in, modes_out)

time: 1010 us -> 978 us (0.968)
  waiting for transfers between devices: 288 us -> 234 us
  blocking collectives: 291 us -> 332 us
  local copies, waits for them, and re-layouts: 264 us -> 240 us
    all_to_all x1 -> x0, waiting for transfers between devices: 184 us -> none  [shards(): lax.all_to_all(mirrored, 'wave', split_axis=4, concat_axis=2, tiled=True)]
    ppermute x0 -> x3, waiting for transfers between devices: none -> 122 us  [try_all_the_tracks(): lax.ppermute(v_next, across, [(w, w ^ m) for w in range(t_next)])]
    another operation x2 -> x7, local copies, waits for them, and re-layouts: 26.6 us -> 81 us
    all_to_all x2 -> x0, local copies, waits for them, and re-layouts: 50.5 us -> none  [shards(): lax.all_to_all(mirrored, 'wave', split_axis=4, concat_axis=2, tiled=True)]
    all_to_all x1, blocking collectives: 189 us -> 231 us  [shards(): lax.all_to_all(grid_coeffs, 'wave', split_axis=2, concat_axis=4, tiled=True)]
    convert_element_type x1 -> x0, local copies, waits for them, and re-layouts: 34.4 us -> none  [shards(): mirrored = (mirror_part.astype(jnp.float32) + hemi_sign * fourier_rows.as...]
    unnamed x20 -> x18, local copies, waits for them, and re-layouts: 32.8 us -> 0.04 us
    gather x0 -> x12, local copies, waits for them, and re-layouts: none -> 26.4 us
  transfers between devices with their start and end apart: 5 -> 7, of which waited for: 4 -> 5; matrix products, arithmetic and copies ran while one was open for 16% -> 15% of each run, Pallas kernels for 0% -> 0%
where the time goes in v1:
time: 978 us; the launch traced here: 965 us
  blocking collectives  332 us (34%)
  local copies, waits for them, and re-layouts  240 us (25%)
  waiting for transfers between devices  234 us (24%)
  matrix products  77.1 us (8%)
  other arithmetic  55.3 us (6%)
  between operations  14 us (1%)
  starting transfers between devices  13 us (1%)
    all_to_all x1, blocking collectives, shards(): lax.all_to_all(grid_coeffs, 'wave', split_axis=2, concat_axis=4, tiled=True)  231 us
    ppermute x3, waiting for transfers between devices, try_all_the_tracks(): lax.ppermute(v_next, across, [(w, w ^ m) for w in range(t_next)])  122 us
    all_to_all x1, blocking collectives, shards(): lax.all_to_all(solved, 'level', split_axis=3, concat_axis=0, tiled=True)  101 us
    all_to_all x1, waiting for transfers between devices, shards(): lax.all_to_all(spectral, 'level', split_axis=0, concat_axis=3, tiled=True)  85.8 us
    another operation x7, local copies, waits for them, and re-layouts  81 us
    ppermute x2, waiting for transfers between devices, partner(): return lax.ppermute(value, axis, pairs)  26.4 us
    gather x12, local copies, waits for them, and re-layouts  26.4 us
    all_to_all x2, local copies, waits for them, and re-layouts, shards(): lax.all_to_all(solved, 'level', split_axis=3, concat_axis=0, tiled=True)  24.2 us
  transfers between devices with their start and end apart: 7, of which 5 were waited for; matrix products, arithmetic and copies ran while one was open for 15% of the time, Pallas kernels for 0%

profile of v1, /device:TPU:0, one launch (start us, length us, event | category | flops | bytes accessed | tf_op | source)
XLA Modules:
  0.0 965.4 jit_solution(4368614038270985137)
XLA Ops:
  6.5 14.1 %multiply_convert_fusion.4 = (bf16[1536,512]{1,0:T(8,128)(2,1)S(1)}, bf16[1536,512]{1,0:T(8,128)(2,1)S(1)}) fusion(s32[512]{0:T(512)} %param.9), kind=kLoop, calls=%fused_computation.32 | loop fusion | flops 11010048 | bytes 3147776 | tf_op jit(solution)/shard_map/convert
  20.7 0.8 sine_multiply_fusion
  21.5 18.9 %fusion.13 = bf16[64,64,1024]{2,1,0:T(8,128)(2,1)} fusion(bf16[64,1,64,1536]{3,2,1,0:T(8,128)(2,1)} %param.7, f32[64]{0:T(128)S(1)} %sine_multiply_fusion, bf16[1536,512]{1,0:T(8,128)(2,1)S(1)} %get-tuple-element.26, bf16[1536,512]{1,0:T(8,128)(2,1)S(1)} %get-tuple-element.25), kind=kOutput, calls=%fused_computation.25 | convolution fusion | flops 12920553472 | bytes 24117504 | tf_op jit(solution)/shard_map/lhrg,gk->lhrk/dot_general | solution.py:119
  40.4 14.5 %reshape.165 = bf16[64,1,64,2,512]{4,3,2,0,1:T(2,128)(2,1)} reshape(bf16[64,64,1024]{2,1,0:T(8,128)(2,1)} %fusion.13) | data formatting | bytes 16777216 | tf_op jit(solution)/shard_map/reshape | solution.py:122
  54.9 9.0 copy.79
  64.5 13.1 %collective-permute-done = bf16[64,1,64,2,512]{4,2,3,0,1:T(8,128)(2,1)} collective-permute-done((bf16[64,1,64,2,512]{4,2,3,0,1:T(8,128)(2,1)}, bf16[64,1,64,2,512]{4,2,3,0,1:T(8,128)(2,1)}, u32[]{:S(2)}, u32[]{:S(2)}) %collective-permute-start) | collective-permute-done | bytes 8388640 | tf_op jit(solution)/shard_map/ppermute | solution.py:43
  77.6 12.1 %add_convert_fusion = bf16[64,1,64,2,512]{4,2,3,0,1:T(8,128)(2,1)} fusion(bf16[64,1,64,2,512]{4,2,3,0,1:T(8,128)(2,1)} %collective-permute-done, f32[]{:T(128)S(6)} %sub.3, bf16[64,1,64,2,512]{4,3,2,0,1:T(2,128)(2,1)} %reshape.165), kind=kLoop, calls=%fused_computation.14 | loop fusion | flops 20971520 | bytes 25165828 | tf_op jit(solution)/shard_map/convert_element_type | solution.py:128
  89.7 12.9 %reshape.166 = bf16[64,1,64,2,4,128]{5,4,2,3,0,1:T(4,128)(2,1)} reshape(bf16[64,1,64,2,512]{4,2,3,0,1:T(8,128)(2,1)} %add_convert_fusion) | data formatting | bytes 16777216 | tf_op jit(solution)/shard_map/reshape | solution.py:12
  102.6 28.6 %constant_dynamic-slice_fusion.5 = (bf16[64,1,64,2,1,128]{5,4,2,3,0,1:T(2,128)(2,1)}, bf16[64,1,64,2,1,128]{5,4,2,3,0,1:T(2,128)(2,1)S(1)}, bf16[64,1,64,2,1,128...) fusion(bf16[64,1,64,2,4,128]{5,4,2,3,0,1:T(4,128)(2,1)} %reshape.166, s32[]{:T(128)S(6)} %select_n.40, ...), kind=kLoop, calls=%fused_computation.51 | loop fusion | bytes 16777232 | tf_op jit(solution)/shard_map/dynamic-slice
  131.2 3.9 copy.116
  135.1 2.8 collective-permute-start.1
  137.9 6.9 copy.115
  144.8 2.6 collective-permute-start.2
  147.3 7.3 copy.114
  154.8 7.8 copy.117
  162.6 59.1 %collective-permute-done.1 = bf16[64,1,64,2,128]{4,3,2,0,1:T(2,128)(2,1)} collective-permute-done((bf16[64,1,64,2,128]{4,3,2,0,1:T(2,128)(2,1)S(1)}, bf16[64,1,64,2,128]{4,3,2,0,1:T(2,128)(2,1)}, u32[]{:S(2)}, u32[]{:S(2)}) %collective-permute-start.1) | collective-permute-done | bytes 2097184 | tf_op jit(solution)/shard_map/ppermute | solution.py:32
  221.7 62.7 %collective-permute-done.2 = bf16[64,1,64,2,128]{4,3,2,0,1:T(2,128)(2,1)} collective-permute-done((bf16[64,1,64,2,128]{4,3,2,0,1:T(2,128)(2,1)}, bf16[64,1,64,2,128]{4,3,2,0,1:T(2,128)(2,1)}, u32[]{:S(2)}, u32[]{:S(2)}) %collective-permute-start.2) | collective-permute-done | bytes 2097184 | tf_op jit(solution)/shard_map/ppermute | solution.py:32
  284.4 17.6 %pad_maximum_fusion = bf16[4,64,1,64,2,128]{5,4,3,2,1,0:T(2,128)(2,1)} fusion(bf16[1,64,1,64,2,128]{5,4,3,2,1,0:T(2,128)(2,1)} %bitcast.8, bf16[1,64,1,64,2,128]{5,4,3,2,1,0:T(2,128)(2,1)} %bitcast.6, bf16[1,64,1,64,2,128]{5,4,3,2,1,0:T(2,128)(2,1)} %bitcast.4, bf16[1,64,1,64,2,128]{5,4,3,2,1,0:T(2,128)(2,1)S(1)} %bitcast.101), kind=kLoop, calls=%fused_computation.21 | loop fusion | flops 12582912 | bytes 16777216 | tf_op jit(solution)/shard_map/stack | solution.py:35
  301.9 26.4 %while.1 = (s32[]{:T(128)}, bf16[4,64,1,64,2,128]{5,4,3,2,1,0:T(2,128)(2,1)}, s32[4,1]{0,1:T(1,128)S(1)}, bf16[4,64,1,64,2,128]{5,3,0,4,1,2:T(8,128)(2,1)}, s32[]{:T(128)}) while((s32[]{:T(128)}, bf16[4,64,1,64,2,128]{5,4,3,2,1,0:T(2,128)(2,1)}, s32[4,1]{0,1:T(1,128)S(1)}, bf16[4,64,1,64,2,128]{5,3,0,4,1,2:T(8,128)(2,1)}, s32[]{:T(128)}) %tuple.20), condition=%wide.while_cond, body=%wide.while_body.sunk | while | flops 2 | bytes 8389197 | solution.py:36
  302.5 4.0 constant_dynamic-slice_fusion.9
  306.6 1.9 copy_dynamic-update-slice_fusion.2
  309.1 4.0 constant_dynamic-slice_fusion.9
  313.1 2.0 copy_dynamic-update-slice_fusion.2
  315.7 4.0 constant_dynamic-slice_fusion.9
  319.7 2.0 copy_dynamic-update-slice_fusion.2
  322.3 4.0 constant_dynamic-slice_fusion.9
  326.4 2.0 copy_dynamic-update-slice_fusion.2
  328.4 12.1 %copy.86 = bf16[64,256,2,128]{1,0,2,3:T(8,128)(2,1)} copy(bf16[64,256,2,128]{3,1,2,0:T(8,128)(2,1)} %bitcast.99) | data formatting | bytes 16777216 | tf_op jit(solution)/shard_map/reshape.8
  340.5 15.1 %fusion.18 = bf16[128,256,2,64]{1,3,2,0:T(8,128)(2,1)} fusion(f32[128,256]{1,0:T(8,128)S(1)} %fusion.26, bf16[64,256,2,128]{1,0,2,3:T(8,128)(2,1)} %copy.86, bf16[128,1,256,256]{3,2,1,0:T(8,128)(2,1)} %all-gather.2.cloned.1.call-done), kind=kOutput, calls=%fused_computation.26 | convolution fusion | flops 2155872256 | bytes 33685504 | tf_op jit(solution)/shard_map/lhrcs,shrj->sjcl/dot_general | solution.py:71
  355.6 7.1 all-to-all-start
  362.9 4.7 add_divide_fusion
  367.6 85.8 %all-to-all-done = bf16[128,256,2,64]{1,3,2,0:T(8,128)(2,1)} async-done(((bf16[128,256,2,64]{1,3,2,0:T(8,128)(2,1)}), bf16[128,256,2,64]{1,3,2,0:T(8,128)(2,1)}, u32[]{:S(2)}, u32[]{:S(2)}) %all-to-all-start) | async-done | bytes 8388640 | tf_op jit(solution)/shard_map/all_to_all | solution.py:131
  453.5 8.4 copy.87
  461.9 10.4 %convolution_convert_fusion.1 = bf16[64,256,2,128]{3,1,2,0:T(8,128)(2,1)} fusion(bf16[64,256,2,128]{1,3,2,0:T(8,128)(2,1)} %bitcast.97, f32[64,256,128]{2,1,0:T(8,128)} %add_divide_fusion, bf16[128,128]{1,0:T(8,128)(2,1)S(1)} %copy-done, bf16[128,128]{1,0:T(8,128)(2,1)S(1)} %copy-done.6), kind=kOutput, calls=%fused_computation.24 | convolution fusion | flops 2160066560 | bytes 25231360 | tf_op jit(solution)/shard_map/sjck,lk->sjcl/dot_general | solution.py:86
  472.3 21.1 %copy.89 = bf16[64,256,2,128]{1,2,0,3:T(2,128)(2,1)} copy(bf16[64,256,2,128]{3,1,2,0:T(8,128)(2,1)} %convolution_convert_fusion.1) | data formatting | bytes 16777216 | tf_op jit(solution)/shard_map/convert_element_type | solution.py:86
  493.3 100.9 %all_to_all.54 = bf16[64,256,2,128]{1,2,0,3:T(2,128)(2,1)} all-to-all(bf16[64,256,2,128]{1,2,0,3:T(2,128)(2,1)} %copy.89), channel_id=1, replica_groups=mesh['member'=2,'wave'=4,'level'=2,'fld'=2] {'level'}, dimensions={3} | all-to-all | bytes 16777216 | tf_op jit(solution)/shard_map/all_to_all | solution.py:133
  594.3 15.9 %copy.90 = bf16[64,256,2,128]{1,3,2,0:T(8,128)(2,1)} copy(bf16[64,256,2,128]{1,2,0,3:T(2,128)(2,1)} %all_to_all.54) | data formatting | bytes 16777216 | tf_op jit(solution)/shard_map/all_to_all | solution.py:133
  610.2 8.3 copy.91
  618.5 13.3 %convert_bitcast_fusion = bf16[64,1,256,2,128]{2,0,3,4,1:T(8,128)(2,1)} fusion(bf16[128,256,2,64]{1,3,2,0:T(8,128)(2,1)} %bitcast.96, bf16[128,1,256,256]{3,2,1,0:T(8,128)(2,1)} %all-gather.2.cloned.1.call-done), kind=kOutput, calls=%fused_computation.22 | convolution fusion | flops 2151677952 | bytes 33554432 | tf_op jit(solution)/shard_map/sjcl,shrj->lhrcs/dot_general | solution.py:78
  631.8 13.5 %copy.92 = bf16[64,1,256,2,128]{4,0,3,1,2:T(8,128)(2,1)} copy(bf16[64,1,256,2,128]{2,0,3,4,1:T(8,128)(2,1)} %convert_bitcast_fusion) | data formatting | bytes 16777216 | tf_op jit(solution)/shard_map/convert_element_type | solution.py:80
  645.3 231.4 %all_to_all.55 = bf16[64,1,256,2,128]{4,0,3,1,2:T(8,128)(2,1)} all-to-all(bf16[64,1,256,2,128]{4,0,3,1,2:T(8,128)(2,1)} %copy.92), channel_id=1, replica_groups=mesh['member'=2,'wave'=4,'level'=2,'fld'=2] {'wave'}, dimensions={2} | all-to-all | bytes 16777216 | tf_op jit(solution)/shard_map/all_to_all | solution.py:135
  876.7 12.2 %copy.93 = bf16[64,1,256,2,128]{4,2,3,0,1:T(8,128)(2,1)} copy(bf16[64,1,256,2,128]{4,0,3,1,2:T(8,128)(2,1)} %all_to_all.55) | data formatting | bytes 16777216 | tf_op jit(solution)/shard_map/all_to_all | solution.py:135
  888.9 8.4 copy.113
  897.3 13.4 %collective-permute-done.4 = bf16[64,1,64,2,512]{4,2,3,0,1:T(8,128)(2,1)S(1)} collective-permute-done((bf16[64,1,64,2,512]{4,2,3,0,1:T(8,128)(2,1)}, bf16[64,1,64,2,512]{4,2,3,0,1:T(8,128)(2,1)S(1)}, u32[]{:S(2)}, u32[]{:S(2)}) %collective-permute-start.4) | collective-permute-done | bytes 8388640 | tf_op jit(solution)/shard_map/ppermute | solution.py:43
  910.7 5.7 multiply_convert_fusion
  916.5 7.7 copy.95
  924.2 14.5 %reshape.169 = bf16[64,64,1024]{2,1,0:T(8,128)(2,1)} reshape(bf16[64,1,64,2,512]{4,3,2,0,1:T(2,128)(2,1)} %copy.95) | data formatting | bytes 16777216 | tf_op jit(solution)/shard_map/reshape.11
  938.7 19.4 %fusion.10 = bf16[64,1,64,1536]{3,2,1,0:T(8,128)(2,1)} fusion(bf16[64,64,1024]{2,1,0:T(8,128)(2,1)} %reshape.169, bf16[1536,512]{1,0:T(8,128)(2,1)S(1)} %copy-done.5, bf16[1536,512]{1,0:T(8,128)(2,1)S(1)} %copy-done.3), kind=kOutput, calls=%fused_computation.19 | convolution fusion | flops 12897484800 | bytes 24117248 | tf_op jit(solution)/shard_map/lhrk,gk->lhrg/dot_general | solution.py:141
  (36 shorter events, 3.3 us)
Async XLA Ops:
  6.5 455.4 %copy-start = (bf16[128,128]{1,0:T(8,128)(2,1)S(1)}, bf16[128,128]{1,0:T(8,128)(2,1)}, u32[]{:S(2)}) copy-start(bf16[128,128]{1,0:T(8,128)(2,1)} %param.13) | copy-start | bytes 98308
  6.5 334.0 %all-gather.2.cloned.1.call-start = ((), (), s32[]{:S(2)}) async-start(), calls=%async_computation.3 | async-start | bytes 25165824 | tf_op jit(solution)/shard_map/all_gather | solution.py:114
  20.6 19.8 %copy-start.2 = (bf16[1536,512]{1,0:T(8,128)(2,1)}, bf16[1536,512]{1,0:T(8,128)(2,1)S(1)}, u32[]{:S(2)}) copy-start(bf16[1536,512]{1,0:T(8,128)(2,1)S(1)} %get-tuple-element.25) | copy-start | bytes 4718596
  20.7 19.8 %copy-start.4 = (bf16[1536,512]{1,0:T(8,128)(2,1)}, bf16[1536,512]{1,0:T(8,128)(2,1)S(1)}, u32[]{:S(2)}) copy-start(bf16[1536,512]{1,0:T(8,128)(2,1)S(1)} %get-tuple-element.26) | copy-start | bytes 4718596
  64.0 13.6 %collective-permute-start = (bf16[64,1,64,2,512]{4,2,3,0,1:T(8,128)(2,1)}, bf16[64,1,64,2,512]{4,2,3,0,1:T(8,128)(2,1)}, u32[]{:S(2)}, u32[]{:S(2)}) collective-permute-start(bf16[64,1,64,2,512]{4,2,3,0,1:T(8,128)(2,1)} %copy.79), channel_id=1, source_target_pairs={{0,1},{1,0},{2,3},{3,2},{4,5},{5,4},{6,7},{7,6},{8,9},{9,8},{10,11... | collective-permute-start | bytes 25165832 | tf_op jit(solution)/shard_map/ppermute | solution.py:43
  131.2 23.4 %copy-start.7 = (s32[512]{0:T(512)S(1)}, s32[512]{0:T(512)}, u32[]{:S(2)}) copy-start(s32[512]{0:T(512)} %param.9) | copy-start | bytes 6148
  135.1 86.6 %collective-permute-start.1 = (bf16[64,1,64,2,128]{4,3,2,0,1:T(2,128)(2,1)S(1)}, bf16[64,1,64,2,128]{4,3,2,0,1:T(2,128)(2,1)}, u32[]{:S(2)}, u32[]{:S(2)}) collective-permute-start(bf16[64,1,64,2,128]{4,3,2,0,1:T(2,128)(2,1)S(1)} %bitcast.102), channel_id=1, source_target_pairs={{0,4},{4,0},{8,12},{12,8},{1,5},{5,1},{9,13},{13,9},{2,6},{6,2},{1... | collective-permute-start | bytes 6291464 | tf_op jit(solution)/shard_map/ppermute | solution.py:32
  144.8 139.6 %collective-permute-start.2 = (bf16[64,1,64,2,128]{4,3,2,0,1:T(2,128)(2,1)}, bf16[64,1,64,2,128]{4,3,2,0,1:T(2,128)(2,1)}, u32[]{:S(2)}, u32[]{:S(2)}) collective-permute-start(bf16[64,1,64,2,128]{4,3,2,0,1:T(2,128)(2,1)} %bitcast.89), channel_id=1, source_target_pairs={{0,8},{4,12},{8,0},{12,4},{1,9},{5,13},{9,1},{13,5},{2,10},{6,14},... | collective-permute-start | bytes 6291464 | tf_op jit(solution)/shard_map/ppermute | solution.py:32
  154.6 129.8 %collective-permute-start.3 = (bf16[64,1,64,2,128]{4,3,2,0,1:T(2,128)(2,1)}, bf16[64,1,64,2,128]{4,3,2,0,1:T(2,128)(2,1)}, u32[]{:S(2)}, u32[]{:S(2)}) collective-permute-start(bf16[64,1,64,2,128]{4,3,2,0,1:T(2,128)(2,1)} %bitcast.88), channel_id=1, source_target_pairs={{0,12},{4,8},{8,4},{12,0},{1,13},{5,9},{9,5},{13,1},{2,14},{6,10},... | collective-permute-start | bytes 6291464 | tf_op jit(solution)/shard_map/ppermute | solution.py:32
  355.6 7.3 copy-start.8
  355.6 97.9 %all-to-all-start = ((bf16[128,256,2,64]{1,3,2,0:T(8,128)(2,1)}), bf16[128,256,2,64]{1,3,2,0:T(8,128)(2,1)}, u32[]{:S(2)}, u32[]{:S(2)}) async-start(bf16[128,256,2,64]{1,3,2,0:T(8,128)(2,1)} %fusion.18), calls=%async_computation | async-start | bytes 16777216 | tf_op jit(solution)/shard_map/all_to_all | solution.py:131
  453.5 8.5 copy-start.6
  897.3 13.4 %collective-permute-start.4 = (bf16[64,1,64,2,512]{4,2,3,0,1:T(8,128)(2,1)}, bf16[64,1,64,2,512]{4,2,3,0,1:T(8,128)(2,1)S(1)}, u32[]{:S(2)}, u32[]{:S(2)}) collective-permute-start(bf16[64,1,64,2,512]{4,2,3,0,1:T(8,128)(2,1)} %bitcast.100), channel_id=1, source_target_pairs={{0,1},{1,0},{2,3},{3,2},{4,5},{5,4},{6,7},{7,6},{8,9},{9,8},{10,11... | collective-permute-start | bytes 25165832 | tf_op jit(solution)/shard_map/ppermute | solution.py:43
  924.2 14.5 %copy-start.3 = (bf16[1536,512]{1,0:T(8,128)(2,1)S(1)}, bf16[1536,512]{1,0:T(8,128)(2,1)}, u32[]{:S(2)}) copy-start(bf16[1536,512]{1,0:T(8,128)(2,1)} %copy-done.2) | copy-start | bytes 4718596
  924.2 14.5 %copy-start.5 = (bf16[1536,512]{1,0:T(8,128)(2,1)S(1)}, bf16[1536,512]{1,0:T(8,128)(2,1)}, u32[]{:S(2)}) copy-start(bf16[1536,512]{1,0:T(8,128)(2,1)} %copy-done.4) | copy-start | bytes 4718596
  938.7 19.4 %copy-start.1 = (bf16[128,128]{1,0:T(8,128)(2,1)S(1)}, bf16[128,128]{1,0:T(8,128)(2,1)}, u32[]{:S(2)}) copy-start(bf16[128,128]{1,0:T(8,128)(2,1)} %param.13) | copy-start | bytes 98308
Sparse Core Ops, SparseCore 0:
  64.6 201.2 all-gather.1
